TPU v7x, 32 devices: a whole 2x2x4 slice. The times are simulated.
32 devices in a mesh: grp: 2 (over y), lat: 4 (over z), chan: 2 (over x), pair: 2 (over core).
Axes of the slice: x: 2, y: 2, z: 4, core: 2. Of those that a mesh axis runs over, the one named last changes fastest.
Arguments:
- grid_field: bfloat16 [4, 352, 256, 1440], P(('grp', 'pair'), 'lat', 'chan'), parts along dimension 0, may hold values from -6 to 6
- legendre: bfloat16 [2, 32, 12, 352, 192], P('pair', None, None, 'lat'), may hold values from -0.3125 to 0.3125
- owned_blocks: int32 [32], replicated, may hold values from 0 to 31, as said below
Outputs:
- spectrum: bfloat16 [32, 4, 12, 192, 512], P('lat', ('grp', 'pair'), None, None, 'chan'), parts along dimension 1
There are 2 independent parts, one for each index of `grp`. A program takes and returns all parts, laid end to end along the dimension named above; an argument that names none is the same for every part. Nothing has to cross between parts.
Inputs may be any that keep to these rules, and one draw needn't show every extreme that they name: `owned_blocks`: every block number appears exactly once; slots 2q and 2q + 1 hold two blocks whose numbers add up to 31.
All inputs are finite; a program needn't handle non-finite values.
Results may differ from a plain program's by a relative error of at most 0.009.
Values may be sent and summed in bfloat16 or wider, within the bound.
A program may use at most 320 MiB of HBM per device.

v0:
```python
import math

import jax
import jax.numpy as jnp
from jax import lax
from jax.sharding import PartitionSpec as P

L = 384
NB = 32
MB = 12
KMAX = 192


def swapped(value, axis, distance):
    mask = 2**distance
    pairs = [(source, source ^ mask) for source in range(lax.axis_size(axis))]
    return lax.ppermute(value, axis, pairs)


def fourier_table(order_count, lon_count):
    orders = jnp.arange(order_count, dtype=jnp.int32)
    points = jnp.arange(lon_count, dtype=jnp.int32)
    phase_index = orders[:, None] * points[None, :] % lon_count
    angles = phase_index.astype(jnp.float32) * (2.0 * math.pi / lon_count)
    scaling = 1.0 / math.sqrt(lon_count)
    return (jnp.stack([jnp.cos(angles), -jnp.sin(angles)], axis=1) * scaling).astype(jnp.bfloat16)


def contract_blocks(tables, folded, picked):
    table_rows = jnp.take(tables, picked, axis=0)
    value_rows = jnp.take(folded, picked, axis=0)
    return jnp.einsum("bjtk,bjtx->bjkx", table_rows, value_rows, preferred_element_type=jnp.float32)


def mask_rows(summed, blocks):
    limits = KMAX - MB // 2 * blocks
    row_index = jnp.arange(summed.shape[2], dtype=jnp.int32)
    inside = row_index[None, :] < limits[:, None]
    return jnp.where(inside[:, None, :, None], summed, jnp.zeros_like(summed))


def per_device(grid_field, legendre, owned_blocks):
    lat_count = lax.axis_size("lat")
    slots_mine = owned_blocks.shape[0] // lat_count
    wave_table = fourier_table(L, grid_field.shape[3])
    local_modes = jnp.einsum(
        "mrn,tcn->mtcr", wave_table, grid_field[0], preferred_element_type=jnp.float32
    ).astype(jnp.bfloat16)
    band_rows = local_modes.shape[1]
    columns = 2 * local_modes.shape[2]
    local_modes = local_modes.reshape(NB, MB, band_rows, columns)
    mirrored = swapped(local_modes, "pair", 0)
    parity_sign = 1.0 - 2.0 * lax.axis_index("pair").astype(jnp.float32)
    folded = (mirrored.astype(jnp.float32) + parity_sign * local_modes.astype(jnp.float32)).astype(
        jnp.bfloat16
    )
    tables = legendre[0]
    first_slot = lax.axis_index("lat") * slots_mine
    my_blocks = lax.dynamic_slice_in_dim(owned_blocks, first_slot, slots_mine)
    summed = lax.psum_scatter(
        contract_blocks(tables, folded, owned_blocks).astype(jnp.bfloat16),
        "lat",
        scatter_dimension=0,
        tiled=True,
    ).astype(jnp.float32)
    result = mask_rows(summed, my_blocks)
    return result.astype(jnp.bfloat16)[:, None]


def solution(mesh):
    return jax.shard_map(
        per_device,
        mesh=mesh,
        in_specs=(P(("grp", "pair"), "lat", "chan", None), P("pair", None, None, "lat", None), P()),
        out_specs=P("lat", ("grp", "pair"), None, None, "chan"),
        check_vma=False,
    )
```

profile of v0, /device:TPU:0, one launch (start us, length us, event | category | flops | bytes accessed | tf_op | source)
XLA Modules:
  0.0 888.2 jit_solution(1636585176764811102)
XLA Ops:
  6.5 0.0 reduce-scatter.4.cloned.1.call-start
  6.5 9.2 %sine_negate_fusion = (f32[384,1,1440]{0,2,1:T(8,128)S(1)}, f32[384,1,1440]{0,2,1:T(8,128)S(1)}) fusion(), kind=kLoop, calls=%fused_computation.23 | loop fusion | flops 5529600 | bytes 4423680 | tf_op jit(solution)/shard_map/neg | solution.py:26
  15.7 33.4 %convert_bitcast_fusion = bf16[384,88,128,2]{2,0,1,3:T(8,128)(2,1)} fusion(bf16[1,88,128,1440]{2,3,1,0:T(8,128)(2,1)} %param.3, f32[384,1,1440]{0,2,1:T(8,128)S(1)} %get-tuple-element.5, f32[384,1,1440]{0,2,1:T(8,128)S(1)} %get-tuple-element.6), kind=kOutput, calls=%fused_computation.10 | convolution fusion | flops 24926134272 | bytes 54165504 | tf_op jit(solution)/shard_map/mrn,tcn->mtcr/dot_general | solution.py:46
  49.2 42.0 %copy.8 = bf16[384,88,128,2]{1,3,2,0:T(2,128)(2,1)} copy(bf16[384,88,128,2]{2,0,1,3:T(8,128)(2,1)} %convert_bitcast_fusion) | data formatting | bytes 34603008 | tf_op jit(solution)/shard_map/convert_element_type | solution.py:48
  91.2 0.0 copy-start
  91.2 27.5 %copy.9 = bf16[32,12,88,256]{3,2,1,0:T(8,128)(2,1)} copy(bf16[32,12,88,256]{2,3,1,0:T(8,128)(2,1)} %bitcast.20) | data formatting | bytes 34603008 | tf_op jit(solution)/shard_map/reshape | solution.py:51
  118.7 0.5 collective-permute-start
  119.1 0.0 copy-done
  119.2 13.4 %gather_fusion = bf16[32,12,88,192]{3,2,1,0:T(8,128)(2,1)} fusion(bf16[32,12,88,192]{3,2,1,0:T(8,128)(2,1)} %bitcast.22, s32[1024]{0:T(1024)S(1)} %pad_clamp_fusion), kind=kCustom, calls=%fused_computation | custom fusion | bytes 25952384 | tf_op jit(solution)/shard_map/jit(_take)/gather | solution.py:30
  132.6 12.4 %collective-permute-done = bf16[32,12,88,256]{3,2,1,0:T(8,128)(2,1)} collective-permute-done((bf16[32,12,88,256]{3,2,1,0:T(8,128)(2,1)}, bf16[32,12,88,256]{3,2,1,0:T(8,128)(2,1)}, u32[]{:S(2)}, u32[]{:S(2)}) %collective-permute-start) | collective-permute-done | bytes 17301536 | tf_op jit(solution)/shard_map/ppermute | solution.py:17
  145.0 27.4 %copy.10 = bf16[32,12,88,256]{2,3,1,0:T(8,128)(2,1)} copy(bf16[32,12,88,256]{3,2,1,0:T(8,128)(2,1)} %collective-permute-done) | data formatting | bytes 34603008 | tf_op jit(solution)/shard_map/ppermute | solution.py:17
  172.4 29.3 %add_convert_fusion = bf16[32,12,88,256]{2,3,1,0:T(8,128)(2,1)} fusion(bf16[32,12,88,256]{2,3,1,0:T(8,128)(2,1)} %bitcast.21, bf16[32,12,88,256]{2,3,1,0:T(8,128)(2,1)} %copy.10, f32[]{:T(128)S(6)} %sub.7), kind=kLoop, calls=%fused_computation.2 | loop fusion | flops 43253760 | bytes 51904516 | tf_op jit(solution)/shard_map/convert_element_type | solution.py:54
  201.7 18.3 %gather_fusion.1 = bf16[32,12,88,256]{2,3,1,0:T(8,128)(2,1)} fusion(bf16[32,12,88,256]{2,3,1,0:T(8,128)(2,1)} %add_convert_fusion, s32[1024]{0:T(1024)S(1)} %pad_clamp_fusion), kind=kCustom, calls=%fused_computation.1 | custom fusion | bytes 34603136 | tf_op jit(solution)/shard_map/jit(_take)/gather | solution.py:31
  220.0 28.7 %fusion.5 = bf16[32,12,192,256]{3,2,1,0:T(8,128)(2,1)} fusion(bf16[32,12,88,256]{2,3,1,0:T(8,128)(2,1)} %gather_fusion.1, pred[32]{0:T(512)(128)(4,1)S(1)} %compare_and_fusion, bf16[32,12,88,192]{3,2,1,0:T(8,128)(2,1)} %gather_fusion), kind=kOutput, calls=%fused_computation.8 | convolution fusion | flops 3355901952 | bytes 68026400 | tf_op jit(solution)/shard_map/bjtk,bjtx->bjkx/dot_general | solution.py:32
  248.7 0.0 reduce-scatter.4.cloned.1.call-update
  248.8 0.1 multiply_subtract_fusion
  248.9 0.1 iota_compare_fusion
  248.9 622.0 %reduce-scatter.4.cloned.1.call-done = bf16[8,12,192,256]{3,2,1,0:T(8,128)(2,1)} async-done(((bf16[32,12,192,256]{3,2,1,0:T(8,128)(2,1)}), bf16[8,12,192,256]{3,2,1,0:T(8,128)(2,1)}) %reduce-scatter.4.cloned.1.call-update) | async-done | bytes 9437200
  870.9 10.5 %fusion.13 = bf16[8,1,12,192,256]{4,3,2,1,0:T(8,128)(2,1)} fusion(bf16[8,12,192,256]{3,2,1,0:T(8,128)(2,1)} %reduce-scatter.4.cloned.1.call-done, pred[8,192]{1,0:T(8,128)(4,1)S(1)} %iota_compare_fusion), kind=kLoop, calls=%fused_computation.14 | loop fusion | flops 14155776 | bytes 18875904 | tf_op jit(solution)/shard_map/broadcast_in_dim | solution.py:67
  (3 shorter events, 0.0 us)
Async XLA Ops:
  6.5 864.3 %reduce-scatter.4.cloned.1.call-start = ((), (), s32[]{:S(2)}) async-start(), calls=%async_computation.1 | async-start | bytes 47185920
  91.2 28.0 %copy-start = (s32[32]{0:T(128)S(1)}, s32[32]{0:T(128)}, u32[]{:S(2)}) copy-start(s32[32]{0:T(128)} %param.5) | copy-start | bytes 388
  118.7 26.4 %collective-permute-start = (bf16[32,12,88,256]{3,2,1,0:T(8,128)(2,1)}, bf16[32,12,88,256]{3,2,1,0:T(8,128)(2,1)}, u32[]{:S(2)}, u32[]{:S(2)}) collective-permute-start(bf16[32,12,88,256]{3,2,1,0:T(8,128)(2,1)} %copy.9), channel_id=1, source_target_pairs={{0,1},{1,0},{2,3},{3,2},{4,5},{5,4},{6,7},{7,6},{8,9},{9,8},{10,11... | collective-permute-start | bytes 51904520 | tf_op jit(solution)/shard_map/ppermute | solution.py:17
Sparse Core Ops, SparseCore 0:
  248.9 621.9 reduce-scatter.3
where the time goes:
time: 891 us; the launch traced here: 888 us
  waiting for transfers between devices  634 us (71%)
  local copies, waits for them, and re-layouts  129 us (14%)
  matrix products  62.2 us (7%)
  other arithmetic  49.2 us (6%)
  between operations  13.4 us (2%)
    unnamed x2, waiting for transfers between devices  622 us
    convert_element_type x1, local copies, waits for them, and re-layouts, per_device(): local_modes = jnp.einsum('mrn,tcn->mtcr', wave_table, grid_field[0], pref...  42 us
    dot_general x1, matrix products, per_device(): jnp.einsum('mrn,tcn->mtcr', wave_table, grid_field[0], preferred_element_...  33.4 us
    convert_element_type x1, other arithmetic, per_device(): (mirrored.astype(jnp.float32) + parity_sign * local_modes.astype(jnp.floa...  29.3 us
    dot_general x1, matrix products, contract_blocks(): jnp.einsum('bjtk,bjtx->bjkx', table_rows, value_rows, preferred_element_t...  28.7 us
    reshape x1, local copies, waits for them, and re-layouts, per_device(): local_modes = local_modes.reshape(NB, MB, band_rows, columns)  27.5 us
    ppermute x1, local copies, waits for them, and re-layouts, swapped(): return lax.ppermute(value, axis, pairs)  27.4 us
    gather x1, local copies, waits for them, and re-layouts, contract_blocks(): value_rows = jnp.take(folded, picked, axis=0)  18.3 us
  transfers between devices with their start and end apart: 2, of which 2 were waited for; matrix products, arithmetic and copies ran while one was open for 2% of the time, Pallas kernels for 0%

commit v1 on v0

v1 whole, which is shorter than its diff:
```python
import functools
import math

import jax
import jax.numpy as jnp
from jax import lax
from jax.experimental import pallas as pl
from jax.experimental.pallas import tpu as pltpu
from jax.sharding import PartitionSpec as P


def swapped(value, axis, distance):
    mask = 2**distance
    pairs = [(source, source ^ mask) for source in range(lax.axis_size(axis))]
    return lax.ppermute(value, axis, pairs)


def trig(index, lon_count):
    angles = (index % lon_count).astype(jnp.float32) * (2.0 * math.pi / lon_count)
    return jnp.cos(angles), jnp.sin(angles)


def wave_rows(base, step):
    cos_a, sin_a = (v[..., None, :] for v in base)
    cos_b, sin_b = step
    cos_sum = cos_a * cos_b - sin_a * sin_b
    sin_sum = sin_a * cos_b + cos_a * sin_b
    return jnp.stack([cos_sum, -sin_sum], axis=-2).astype(jnp.bfloat16)


def pack_kernel(kmax, half, blocks, total, meta, lo_ref, hi_ref, own_ref, mir_ref, out_ref):
    pair = pl.program_id(0)
    lo = meta[pair]
    sign = meta[pl.num_programs(0)].astype(jnp.float32)
    limit = kmax - half * lo
    width = out_ref.shape[3]
    place = lax.broadcasted_iota(jnp.int32, (width, kmax), 0)
    row = lax.broadcasted_iota(jnp.int32, (width, kmax), 1)
    pick_lo = ((place == row) & (place < limit)).astype(jnp.float32).astype(jnp.bfloat16)
    pick_hi = ((place == row + limit) & (place < total)).astype(jnp.float32).astype(jnp.bfloat16)
    nt = (((1,), (1,)), ((), ()))
    for j in range(lo_ref.shape[1]):
        tables = [
            lax.dot_general(pick, ref[0, j], nt, preferred_element_type=jnp.float32).astype(jnp.bfloat16)
            for pick, ref in ((pick_lo, lo_ref), (pick_hi, hi_ref))
        ]
        for r in range(out_ref.shape[2]):
            acc = None
            for side in range(2):
                own = own_ref[0, side, j, r].astype(jnp.float32)
                mir = mir_ref[0, side, j, r].astype(jnp.float32)
                folded = (mir + sign * own).astype(jnp.bfloat16)
                term = jnp.dot(tables[side], folded, preferred_element_type=jnp.float32)
                acc = term if acc is None else acc + term
            out_ref[0, j, r] = acc.astype(jnp.bfloat16)


def pack(tables, own, mirrored, lows, sign, orders_step):
    nb, mb, band, kmax = tables.shape
    pairs, _, _, parts, _, chan = own.shape
    half = mb // 2
    total = 2 * kmax - half * (nb - 1)
    width = -(-total // 8) * 8
    meta = jnp.concatenate([lows, sign[None]])
    value_spec = pl.BlockSpec(
        (1, 2, orders_step, parts, band, chan), lambda p, j, m: (p, 0, j, 0, 0, 0)
    )
    return pl.pallas_call(
        functools.partial(pack_kernel, kmax, half, nb, total),
        out_shape=jax.ShapeDtypeStruct((pairs, mb, parts, width, chan), jnp.bfloat16),
        grid_spec=pltpu.PrefetchScalarGridSpec(
            num_scalar_prefetch=1,
            grid=(pairs, mb // orders_step),
            in_specs=[
                pl.BlockSpec((1, orders_step, band, kmax), lambda p, j, m: (m[p], j, 0, 0)),
                pl.BlockSpec((1, orders_step, band, kmax), lambda p, j, m: (nb - 1 - m[p], j, 0, 0)),
                value_spec,
                value_spec,
            ],
            out_specs=pl.BlockSpec(
                (1, orders_step, parts, width, chan), lambda p, j, m: (p, j, 0, 0, 0)
            ),
        ),
        cost_estimate=pl.CostEstimate(
            flops=4 * own.size * width,
            bytes_accessed=4 * own.size + 4 * pairs * mb * band * kmax + 2 * pairs * mb * parts * width * chan,
            transcendentals=0,
        ),
        name="pack",
    )(meta, tables, tables, own, mirrored)


def unpack_kernel(nb, half, total, meta, sum_ref, *rest):
    out_ref = rest[-1]
    block = meta[pl.program_id(0)]
    kmax, columns = out_ref.shape[3:]
    width, chan = sum_ref.shape[2:]
    low = jnp.minimum(block, nb - 1 - block)
    shift = jnp.where(2 * block < nb, 0, kmax - half * low)
    limit = kmax - half * block
    row = lax.broadcasted_iota(jnp.int32, (kmax, width), 0)
    place = lax.broadcasted_iota(jnp.int32, (kmax, width), 1)
    pick = ((place == row + shift) & (row < limit)).astype(jnp.float32).astype(jnp.bfloat16)
    source = lax.broadcasted_iota(jnp.int32, (chan, columns), 0)
    target = lax.broadcasted_iota(jnp.int32, (chan, columns), 1)
    parts = sum_ref.shape[1]
    spread = [
        (target == parts * source + r).astype(jnp.float32).astype(jnp.bfloat16) for r in range(parts)
    ]
    for j in range(sum_ref.shape[0]):
        acc = None
        for r in range(parts):
            rows = jnp.dot(pick, sum_ref[j, r], preferred_element_type=jnp.float32).astype(jnp.bfloat16)
            term = jnp.dot(rows, spread[r], preferred_element_type=jnp.float32)
            acc = term if acc is None else acc + term
        out_ref[0, 0, j] = acc.astype(jnp.bfloat16)


def unpack(summed, blocks, previous, first, slots, kmax, nb, orders_step):
    mb, parts, width, chan = summed.shape
    half = mb // 2
    total = 2 * kmax - half * (nb - 1)
    operands = [blocks, summed]
    in_specs = [pl.BlockSpec((orders_step, parts, width, chan), lambda s, j, m: (j, 0, 0, 0))]
    aliases = {}
    if previous is not None:
        operands.append(previous)
        in_specs.append(pl.BlockSpec(memory_space=pl.ANY))
        aliases = {2: 0}
    return pl.pallas_call(
        functools.partial(unpack_kernel, nb, half, total),
        out_shape=jax.ShapeDtypeStruct((slots, 1, mb, kmax, parts * chan), jnp.bfloat16),
        grid_spec=pltpu.PrefetchScalarGridSpec(
            num_scalar_prefetch=1,
            grid=(2, mb // orders_step),
            in_specs=in_specs,
            out_specs=pl.BlockSpec(
                (1, 1, orders_step, kmax, parts * chan), lambda s, j, m: (first + s, 0, j, 0, 0)
            ),
        ),
        input_output_aliases=aliases,
        cost_estimate=pl.CostEstimate(
            flops=4 * mb * parts * kmax * width * chan,
            bytes_accessed=4 * summed.size + 4 * mb * kmax * parts * chan,
            transcendentals=0,
        ),
        name="unpack",
    )(*operands)


def per_device(grid_field, legendre, owned_blocks):
    lat_count = lax.axis_size("lat")
    tables = legendre[0]
    nb, mb, band, kmax = tables.shape
    field = grid_field[0]
    _, chan, lon = field.shape
    slots = nb // lat_count
    rounds = slots // 2
    orders_step = 3 if mb % 3 == 0 else 1
    sign = 1 - 2 * lax.axis_index("pair").astype(jnp.int32)
    by_pair = owned_blocks.reshape(lat_count, rounds, 2)
    lows = jnp.min(by_pair, axis=2)
    both = jnp.stack([lows, nb - 1 - lows], axis=2)
    points = jnp.arange(lon, dtype=jnp.int32)
    base = trig(both[..., None] * mb % lon * points, lon)
    step = trig(jnp.arange(mb, dtype=jnp.int32)[:, None] * points, lon)
    scale = 1.0 / math.sqrt(lon)
    step = tuple(v * scale for v in step)
    mine = lax.dynamic_slice_in_dim(owned_blocks, lax.axis_index("lat") * slots, slots)
    result = None
    for i in range(rounds):
        waves = wave_rows(tuple(v[:, i] for v in base), step)
        own = jnp.einsum(
            "pbjrn,tcn->pbjrtc", waves, field, preferred_element_type=jnp.float32
        ).astype(jnp.bfloat16)
        mirrored = swapped(own, "pair", 0)
        packed = pack(tables, own, mirrored, lows[:, i], sign, orders_step)
        summed = lax.psum_scatter(packed, "lat", scatter_dimension=0, tiled=True)
        result = unpack(
            summed[0], lax.slice_in_dim(mine, 2 * i, 2 * i + 2), result, 2 * i, slots, kmax, nb, orders_step
        )
    return result


def solution(mesh):
    return jax.shard_map(
        per_device,
        mesh=mesh,
        in_specs=(P(("grp", "pair"), "lat", "chan", None), P("pair", None, None, "lat", None), P()),
        out_specs=P("lat", ("grp", "pair"), None, None, "chan"),
        check_vma=False,
    )
```

time: 891 us -> 443 us (0.50)
  waiting for transfers between devices: 634 us -> 222 us
  Pallas kernels: 0 us -> 115 us
  local copies, waits for them, and re-layouts: 129 us -> 17.4 us
  other arithmetic: 49.2 us -> 8.81 us
    unnamed x2 -> x4, waiting for transfers between devices: 622 us -> 0.07 us
    reduce_scatter x0 -> x4, waiting for transfers between devices: none -> 196 us  [per_device(): summed = lax.psum_scatter(packed, 'lat', scatter_dimension=0, tiled=True)]
    pallas_call x0 -> x8, Pallas kernels: none -> 115 us  [the longest x4 79.5 us: pack(): pl.pallas_call(functools.partial(pack_kernel, kmax, half, nb, total), out...]
    convert_element_type x1 -> x0, local copies, waits for them, and re-layouts: 42 us -> none  [per_device(): local_modes = jnp.einsum('mrn,tcn->mtcr', wave_table, grid_field[0], pref...]
    gather x2 -> x0, local copies, waits for them, and re-layouts: 31.8 us -> none  [the longest x1 18.3 us: contract_blocks(): value_rows = jnp.take(folded, picked, axis=0)]
    convert_element_type x1 -> x0, other arithmetic: 29.3 us -> none  [per_device(): (mirrored.astype(jnp.float32) + parity_sign * local_modes.astype(jnp.floa...]
    ppermute x1 -> x0, local copies, waits for them, and re-layouts: 27.4 us -> none  [swapped(): return lax.ppermute(value, axis, pairs)]
    reshape x1, local copies, waits for them, and re-layouts: 27.5 us -> 0.75 us  [per_device(): by_pair = owned_blocks.reshape(lat_count, rounds, 2)]
  transfers between devices with their start and end apart: 2 -> 8, of which waited for: 2 -> 7; matrix products, arithmetic and copies ran while one was open for 2% -> 12% of each run, Pallas kernels for 0% -> 20%
where the time goes in v1:
time: 443 us; the launch traced here: 440 us
  waiting for transfers between devices  222 us (50%)
  Pallas kernels  115 us (26%)
  matrix products  61.8 us (14%)
  local copies, waits for them, and re-layouts  17.4 us (4%)
  between operations  13.3 us (3%)
  other arithmetic  8.81 us (2%)
    reduce_scatter x4, waiting for transfers between devices, per_device(): summed = lax.psum_scatter(packed, 'lat', scatter_dimension=0, tiled=True)  196 us
    pallas_call x4, Pallas kernels, pack(): pl.pallas_call(functools.partial(pack_kernel, kmax, half, nb, total), out...  79.5 us
    dot_general x4, matrix products, per_device(): jnp.einsum('pbjrn,tcn->pbjrtc', waves, field, preferred_element_type=jnp....  61.8 us
    pallas_call x4, Pallas kernels, unpack(): pl.pallas_call(functools.partial(unpack_kernel, nb, half, total), out_sha...  35.3 us
    ppermute x4, waiting for transfers between devices, swapped(): return lax.ppermute(value, axis, pairs)  25.5 us
  transfers between devices with their start and end apart: 8, of which 7 were waited for; matrix products, arithmetic and copies ran while one was open for 12% of the time, Pallas kernels for 20%

profile of v1, /device:TPU:0, one launch (start us, length us, event | category | flops | bytes accessed | tf_op | source)
XLA Modules:
  0.0 440.3 jit_solution(4312955016026119175)
XLA Ops:
  6.5 0.0 reduce-scatter.11.cloned.1.call-start
  6.5 0.4 sine_multiply_fusion
  7.0 0.7 reshape.164
  7.7 0.2 reduce_min.9
  7.9 0.1 copy.24
  8.0 3.6 fusion.23
  11.7 2.2 subtract_convert_fusion
  13.9 15.1 %fusion = bf16[4,2,12,2,88,128]{5,2,4,3,1,0:T(8,128)(2,1)S(1)} fusion(bf16[1,88,128,1440]{2,3,1,0:T(8,128)(2,1)} %param.3, bf16[4,2,12,1,1440]{4,2,3,1,0:T(8,128)(2,1)} %get-tuple-element.10, bf16[4,2,12,1,1440]{4,2,3,1,0:T(8,128)(2,1)} %get-tuple-element.9), kind=kOutput, calls=%fused_computation | convolution fusion | flops 6229647360 | bytes 37318656 | tf_op jit(solution)/shard_map/pbjrn,tcn->pbjrtc/dot_general | solution.py:173
  29.0 3.1 copy.38.own_ref
  32.1 0.5 collective-permute-start.3
  32.6 0.7 slice_reduce_fusion
  33.3 0.6 pad_add_fusion.3.meta
  33.9 6.0 %collective-permute-done.3.mir_ref = bf16[4,2,12,2,88,128]{5,4,3,2,1,0:T(8,128)(2,1)} collective-permute-done((bf16[4,2,12,2,88,128]{5,4,3,2,1,0:T(8,128)(2,1)}, bf16[4,2,12,2,88,128]{5,4,3,2,1,0:T(8,128)(2,1)}, u32[]{:S(2)}, u32[]{:S(2)}) %collective-permute-start.3) | collective-permute-done | bytes 4325408 | tf_op jit(solution)/shard_map/ppermute | solution.py:15
  39.9 19.9 %pack.7 = bf16[4,12,2,200,128]{4,3,2,1,0:T(8,128)(2,1)} custom-call(s32[5]{0:T(128)} %pad_add_fusion.3.meta, bf16[32,12,88,192]{3,2,1,0:T(8,128)(2,1)} %bitcast.57, bf16[32,12,88,192]{3,2,1,0:T(8,128)(2,1)} %bitcast.58, bf16[4,2,12,2,88,128]{5,4,3,2,1,0:T(8,128)(2,1)} %copy.38.own_ref, bf16[4,2,12,2,88,128]{5,4,3,2,1,0:T(8,128)(2,1)} %collective-permute-done.3.mir_ref), custom_call_target="tpu_custom_call" | custom-call | flops 1730150400 | bytes 16809984 | tf_op jit(solution)/shard_map/pack/pallas_call | solution.py:68
  59.8 0.0 reduce-scatter.11.cloned.1.call-update
  59.8 0.2 reduce-scatter.9.cloned.1.call-start
  60.0 15.8 %fusion.2 = bf16[4,2,12,2,88,128]{5,2,4,3,1,0:T(8,128)(2,1)S(1)} fusion(bf16[1,88,128,1440]{2,3,1,0:T(8,128)(2,1)} %param.3, bf16[4,2,12,1,1440]{4,2,3,1,0:T(8,128)(2,1)S(1)} %get-tuple-element.19, bf16[4,2,12,1,1440]{4,2,3,1,0:T(8,128)(2,1)S(1)} %get-tuple-element.20), kind=kOutput, calls=%fused_computation.2 | convolution fusion | flops 6229647360 | bytes 37318656 | tf_op jit(solution)/shard_map/pbjrn,tcn->pbjrtc/dot_general | solution.py:173
  75.8 1.1 copy.39.own_ref
  77.0 0.0 copy-start.1
  77.0 2.0 copy-done.1
  79.0 0.4 collective-permute-start.2
  79.4 0.6 pad_add_fusion.2.meta
  80.0 6.5 %collective-permute-done.2.mir_ref = bf16[4,2,12,2,88,128]{5,4,3,2,1,0:T(8,128)(2,1)} collective-permute-done((bf16[4,2,12,2,88,128]{5,4,3,2,1,0:T(8,128)(2,1)S(1)}, bf16[4,2,12,2,88,128]{5,4,3,2,1,0:T(8,128)(2,1)}, u32[]{:S(2)}, u32[]{:S(2)}) %collective-permute-start.2) | collective-permute-done | bytes 4325408 | tf_op jit(solution)/shard_map/ppermute | solution.py:15
  86.5 19.9 %pack.6 = bf16[4,12,2,200,128]{4,3,2,1,0:T(8,128)(2,1)} custom-call(s32[5]{0:T(128)} %pad_add_fusion.2.meta, bf16[32,12,88,192]{3,2,1,0:T(8,128)(2,1)} %bitcast.59, bf16[32,12,88,192]{3,2,1,0:T(8,128)(2,1)} %bitcast.60, bf16[4,2,12,2,88,128]{5,4,3,2,1,0:T(8,128)(2,1)} %copy-done.1, bf16[4,2,12,2,88,128]{5,4,3,2,1,0:T(8,128)(2,1)} %collective-permute-done.2.mir_ref), custom_call_target="tpu_custom_call" | custom-call | flops 1730150400 | bytes 16809984 | tf_op jit(solution)/shard_map/pack/pallas_call | solution.py:68
  106.4 0.0 copy-start.5
  106.4 0.0 reduce-scatter.9.cloned.1.call-update
  106.4 0.0 reduce-scatter.7.cloned.1.call-start
  106.5 0.9 copy-done.5
  107.4 0.1 copy-done.6
  107.5 15.1 %fusion.4 = bf16[4,2,12,2,88,128]{5,2,4,3,1,0:T(8,128)(2,1)S(1)} fusion(bf16[1,88,128,1440]{2,3,1,0:T(8,128)(2,1)} %param.3, bf16[4,2,12,1,1440]{4,2,3,1,0:T(8,128)(2,1)S(1)} %copy-done.5, bf16[4,2,12,1,1440]{4,2,3,1,0:T(8,128)(2,1)S(1)} %copy-done.6), kind=kOutput, calls=%fused_computation.4 | convolution fusion | flops 6229647360 | bytes 37318656 | tf_op jit(solution)/shard_map/pbjrn,tcn->pbjrtc/dot_general | solution.py:173
  122.6 0.0 copy-start.9
  122.6 1.1 copy.40.own_ref
  123.7 0.0 copy-start.2
  123.8 2.1 copy-done.2
  125.9 0.4 collective-permute-start.1
  126.2 0.0 copy-done.9
  126.2 0.6 pad_add_fusion.1.meta
  126.9 6.5 %collective-permute-done.1.mir_ref = bf16[4,2,12,2,88,128]{5,4,3,2,1,0:T(8,128)(2,1)} collective-permute-done((bf16[4,2,12,2,88,128]{5,4,3,2,1,0:T(8,128)(2,1)S(1)}, bf16[4,2,12,2,88,128]{5,4,3,2,1,0:T(8,128)(2,1)}, u32[]{:S(2)}, u32[]{:S(2)}) %collective-permute-start.1) | collective-permute-done | bytes 4325408 | tf_op jit(solution)/shard_map/ppermute | solution.py:15
  133.3 19.9 %pack.5 = bf16[4,12,2,200,128]{4,3,2,1,0:T(8,128)(2,1)} custom-call(s32[5]{0:T(128)} %pad_add_fusion.1.meta, bf16[32,12,88,192]{3,2,1,0:T(8,128)(2,1)} %bitcast.61, bf16[32,12,88,192]{3,2,1,0:T(8,128)(2,1)} %bitcast.62, bf16[4,2,12,2,88,128]{5,4,3,2,1,0:T(8,128)(2,1)} %copy-done.2, bf16[4,2,12,2,88,128]{5,4,3,2,1,0:T(8,128)(2,1)} %collective-permute-done.1.mir_ref), custom_call_target="tpu_custom_call" | custom-call | flops 1730150400 | bytes 16809984 | tf_op jit(solution)/shard_map/pack/pallas_call | solution.py:68
  153.3 0.0 reduce-scatter.7.cloned.1.call-update
  153.3 0.3 reduce-scatter.5.cloned.1.call-start
  153.6 0.7 copy-done.3
  154.3 0.1 copy-done.4
  154.4 15.8 %fusion.6 = bf16[4,2,12,2,88,128]{5,2,4,3,1,0:T(8,128)(2,1)S(1)} fusion(bf16[1,88,128,1440]{2,3,1,0:T(8,128)(2,1)} %param.3, bf16[4,2,12,1,1440]{4,2,3,1,0:T(8,128)(2,1)S(1)} %copy-done.3, bf16[4,2,12,1,1440]{4,2,3,1,0:T(8,128)(2,1)S(1)} %copy-done.4), kind=kOutput, calls=%fused_computation.6 | convolution fusion | flops 6229647360 | bytes 37318656 | tf_op jit(solution)/shard_map/pbjrn,tcn->pbjrtc/dot_general | solution.py:173
  170.2 0.0 copy-start.8
  170.2 1.1 copy.41.own_ref
  171.3 0.0 copy-start
  171.3 2.0 copy-done
  173.3 0.4 collective-permute-start
  173.7 0.0 copy-done.8
  173.7 0.6 pad_add_fusion.meta
  174.3 6.5 %collective-permute-done.mir_ref = bf16[4,2,12,2,88,128]{5,4,3,2,1,0:T(8,128)(2,1)} collective-permute-done((bf16[4,2,12,2,88,128]{5,4,3,2,1,0:T(8,128)(2,1)S(1)}, bf16[4,2,12,2,88,128]{5,4,3,2,1,0:T(8,128)(2,1)}, u32[]{:S(2)}, u32[]{:S(2)}) %collective-permute-start) | collective-permute-done | bytes 4325408 | tf_op jit(solution)/shard_map/ppermute | solution.py:15
  180.8 19.9 %pack.4 = bf16[4,12,2,200,128]{4,3,2,1,0:T(8,128)(2,1)} custom-call(s32[5]{0:T(128)} %pad_add_fusion.meta, bf16[32,12,88,192]{3,2,1,0:T(8,128)(2,1)} %bitcast.63, bf16[32,12,88,192]{3,2,1,0:T(8,128)(2,1)} %bitcast.64, bf16[4,2,12,2,88,128]{5,4,3,2,1,0:T(8,128)(2,1)} %copy-done, bf16[4,2,12,2,88,128]{5,4,3,2,1,0:T(8,128)(2,1)} %collective-permute-done.mir_ref), custom_call_target="tpu_custom_call" | custom-call | flops 1730150400 | bytes 16809984 | tf_op jit(solution)/shard_map/pack/pallas_call | solution.py:68
  200.7 0.0 reduce-scatter.5.cloned.1.call-update
  200.7 0.6 copy-done.7
  201.3 0.1 dynamic_slice.3
  201.4 0.7 fusion.30
  202.1 8.8 %unpack.4.rest_0_ = bf16[8,1,12,192,256]{4,3,2,1,0:T(8,128)(2,1)} custom-call(s32[2]{0:T(128)} %get-tuple-element.33.meta, bf16[12,2,200,128]{3,2,1,0:T(8,128)(2,1)} %bitcast.68), custom_call_target="tpu_custom_call" | custom-call | flops 471859200 | bytes 4816896 | tf_op jit(solution)/shard_map/unpack/pallas_call | solution.py:130
  210.9 31.4 %reduce-scatter.9.cloned.1.call-done = bf16[1,12,2,200,128]{4,3,2,1,0:T(8,128)(2,1)} async-done(((bf16[4,12,2,200,128]{4,3,2,1,0:T(8,128)(2,1)}), bf16[1,12,2,200,128]{4,3,2,1,0:T(8,128)(2,1)}) %reduce-scatter.9.cloned.1.call-update) | async-done | bytes 1228816 | tf_op jit(solution)/shard_map/reduce_scatter | solution.py:178
  242.4 8.8 %unpack.5.rest_0_ = bf16[8,1,12,192,256]{4,3,2,1,0:T(8,128)(2,1)} custom-call(s32[2]{0:T(128)} %get-tuple-element.34.meta, bf16[12,2,200,128]{3,2,1,0:T(8,128)(2,1)} %bitcast.65, bf16[8,1,12,192,256]{4,3,2,1,0:T(8,128)(2,1)} %unpack.4.rest_0_), custom_call_target="tpu_custom_call", output_to_operand_aliasing={{}: (2, {})} | custom-call | flops 471859200 | bytes 4816896 | tf_op jit(solution)/shard_map/unpack/pallas_call | solution.py:130
  251.2 82.5 %reduce-scatter.7.cloned.1.call-done = bf16[1,12,2,200,128]{4,3,2,1,0:T(8,128)(2,1)} async-done(((bf16[4,12,2,200,128]{4,3,2,1,0:T(8,128)(2,1)}), bf16[1,12,2,200,128]{4,3,2,1,0:T(8,128)(2,1)}) %reduce-scatter.7.cloned.1.call-update) | async-done | bytes 1228816 | tf_op jit(solution)/shard_map/reduce_scatter | solution.py:178
  333.7 8.8 %unpack.6.rest_0_ = bf16[8,1,12,192,256]{4,3,2,1,0:T(8,128)(2,1)} custom-call(s32[2]{0:T(128)} %get-tuple-element.35.meta, bf16[12,2,200,128]{3,2,1,0:T(8,128)(2,1)} %bitcast.66, bf16[8,1,12,192,256]{4,3,2,1,0:T(8,128)(2,1)} %unpack.5.rest_0_), custom_call_target="tpu_custom_call", output_to_operand_aliasing={{}: (2, {})} | custom-call | flops 471859200 | bytes 4816896 | tf_op jit(solution)/shard_map/unpack/pallas_call | solution.py:130
  342.5 82.4 %reduce-scatter.5.cloned.1.call-done = bf16[1,12,2,200,128]{4,3,2,1,0:T(8,128)(2,1)} async-done(((bf16[4,12,2,200,128]{4,3,2,1,0:T(8,128)(2,1)}), bf16[1,12,2,200,128]{4,3,2,1,0:T(8,128)(2,1)}) %reduce-scatter.5.cloned.1.call-update) | async-done | bytes 1228816 | tf_op jit(solution)/shard_map/reduce_scatter | solution.py:178
  424.9 8.8 %unpack.7 = bf16[8,1,12,192,256]{4,3,2,1,0:T(8,128)(2,1)} custom-call(s32[2]{0:T(128)} %get-tuple-element.36.meta, bf16[12,2,200,128]{3,2,1,0:T(8,128)(2,1)} %bitcast.67, bf16[8,1,12,192,256]{4,3,2,1,0:T(8,128)(2,1)} %unpack.6.rest_0_), custom_call_target="tpu_custom_call", output_to_operand_aliasing={{}: (2, {})} | custom-call | flops 471859200 | bytes 4816896 | tf_op jit(solution)/shard_map/unpack/pallas_call | solution.py:130
  (8 shorter events, 0.1 us)
Async XLA Ops:
  6.5 195.6 %reduce-scatter.11.cloned.1.call-start = ((), (), s32[]{:S(2)}) async-start(), calls=%async_computation.7 | async-start | bytes 6144000 | tf_op jit(solution)/shard_map/reduce_scatter | solution.py:178
  32.1 7.8 %collective-permute-start.3 = (bf16[4,2,12,2,88,128]{5,4,3,2,1,0:T(8,128)(2,1)}, bf16[4,2,12,2,88,128]{5,4,3,2,1,0:T(8,128)(2,1)}, u32[]{:S(2)}, u32[]{:S(2)}) collective-permute-start(bf16[4,2,12,2,88,128]{5,4,3,2,1,0:T(8,128)(2,1)} %copy.38.own_ref), channel_id=1, source_target_pairs={{0,1},{1,0},{2,3},{3,2},{4,5},{5,4},{6,7},{7,6},{8,9},{9,8},{10,11... | collective-permute-start | bytes 12976136 | tf_op jit(solution)/shard_map/ppermute | solution.py:15
  59.8 182.6 %reduce-scatter.9.cloned.1.call-start = ((), (), s32[]{:S(2)}) async-start(), calls=%async_computation.6 | async-start | bytes 6144000 | tf_op jit(solution)/shard_map/reduce_scatter | solution.py:178
  77.0 2.0 copy-start.1
  79.0 7.5 %collective-permute-start.2 = (bf16[4,2,12,2,88,128]{5,4,3,2,1,0:T(8,128)(2,1)S(1)}, bf16[4,2,12,2,88,128]{5,4,3,2,1,0:T(8,128)(2,1)}, u32[]{:S(2)}, u32[]{:S(2)}) collective-permute-start(bf16[4,2,12,2,88,128]{5,4,3,2,1,0:T(8,128)(2,1)S(1)} %copy.39.own_ref), channel_id=1, source_target_pairs={{0,1},{1,0},{2,3},{3,2},{4,5},{5,4},{6,7},{7,6},{8,9},{9,8},{10,11... | collective-permute-start | bytes 12976136 | tf_op jit(solution)/shard_map/ppermute | solution.py:15
  106.4 1.0 copy-start.5
  106.4 1.1 copy-start.6
  106.4 227.3 %reduce-scatter.7.cloned.1.call-start = ((), (), s32[]{:S(2)}) async-start(), calls=%async_computation.5 | async-start | bytes 6144000 | tf_op jit(solution)/shard_map/reduce_scatter | solution.py:178
  122.6 3.6 copy-start.9
  123.7 2.1 copy-start.2
  125.9 7.5 %collective-permute-start.1 = (bf16[4,2,12,2,88,128]{5,4,3,2,1,0:T(8,128)(2,1)S(1)}, bf16[4,2,12,2,88,128]{5,4,3,2,1,0:T(8,128)(2,1)}, u32[]{:S(2)}, u32[]{:S(2)}) collective-permute-start(bf16[4,2,12,2,88,128]{5,4,3,2,1,0:T(8,128)(2,1)S(1)} %copy.40.own_ref), channel_id=1, source_target_pairs={{0,1},{1,0},{2,3},{3,2},{4,5},{5,4},{6,7},{7,6},{8,9},{9,8},{10,11... | collective-permute-start | bytes 12976136 | tf_op jit(solution)/shard_map/ppermute | solution.py:15
  153.3 1.0 copy-start.3
  153.3 1.1 copy-start.4
  153.3 271.6 %reduce-scatter.5.cloned.1.call-start = ((), (), s32[]{:S(2)}) async-start(), calls=%async_computation.4 | async-start | bytes 6144000 | tf_op jit(solution)/shard_map/reduce_scatter | solution.py:178
  170.2 3.5 copy-start.8
  171.3 2.0 copy-start
  173.3 7.5 %collective-permute-start = (bf16[4,2,12,2,88,128]{5,4,3,2,1,0:T(8,128)(2,1)S(1)}, bf16[4,2,12,2,88,128]{5,4,3,2,1,0:T(8,128)(2,1)}, u32[]{:S(2)}, u32[]{:S(2)}) collective-permute-start(bf16[4,2,12,2,88,128]{5,4,3,2,1,0:T(8,128)(2,1)S(1)} %copy.41.own_ref), channel_id=1, source_target_pairs={{0,1},{1,0},{2,3},{3,2},{4,5},{5,4},{6,7},{7,6},{8,9},{9,8},{10,11... | collective-permute-start | bytes 12976136 | tf_op jit(solution)/shard_map/ppermute | solution.py:15
  200.7 0.7 copy-start.7
Sparse Core Ops, SparseCore 0:
  59.9 91.0 reduce-scatter.10
  153.4 88.9 reduce-scatter.8
  244.7 88.9 reduce-scatter.6
  335.9 88.9 reduce-scatter.4
